TPU v7x, 32 devices: a whole 2x2x4 slice. The times are simulated.
32 devices in a mesh: ctx: 8 (over z, x), head: 4 (over y, core).
Axes of the slice: x: 2, y: 2, z: 4, core: 2. Of those that a mesh axis runs over, the one named last changes fastest.
Arguments:
- query: bfloat16 [16384, 8192], P(('ctx', 'head')), as said below
- key: bfloat16 [16384, 1024], P(('ctx', 'head')), as said below
- value: bfloat16 [16384, 1024], P(('ctx', 'head')), may hold values from -6 to 6
- doc_ids: int32 [128], replicated, may hold values from 0 to 20, never falling along the last dimension, each value on 1 to 8 neighbouring positions
- plan: int32 [128], replicated, may hold values from 0 to 127, as said below
Outputs:
- attended: bfloat16 [16384, 8192], P('ctx', 'head')
Inputs may be any that keep to these rules, and one draw needn't show every extreme that they name: `doc_ids`: block ids never fall; each document holds 1 to 8 blocks, one exactly 8. `plan`: A permutation of the 128 blocks. Output positions k * 16 to (k + 1) * 16 - 1 belong to context shard k. Every shard receives 16 blocks; of the blocks j * 16 to (j + 1) * 16 - 1 at most 2 go to one shard, and exactly 2 to some shard. `query`: real values; no structure promised. `key`: real values; no structure promised.
All inputs are finite; a program needn't handle non-finite values.
Results may differ from a plain program's by a relative error of at most 0.0038.
Values may be sent and summed in bfloat16 or wider, within the bound.
A program may use at most 128 MiB of HBM per device.

v0:
```python
import math

import jax
import jax.numpy as jnp
from jax import lax
from jax.sharding import PartitionSpec as P

HD = 128
BLK = 128
MAXDOC = 8


def shifted(shard, axis, by):
    count = lax.axis_size(axis)
    pairs = [(i, i + by) for i in range(count) if 0 <= i + by < count]
    return lax.ppermute(shard, axis, pairs)


def attend(query_set, block_ids, keys_all, values_all, first_block, doc_start, kv_heads, group):
    count = query_set.shape[0]
    q_width = query_set.shape[2]
    scale = 1.0 / math.sqrt(HD)
    positions = jnp.arange(BLK, dtype=jnp.int32)
    causal = positions[None, :] <= positions[:, None]

    def per_block(index, result):
        block = block_ids[index]
        begin = doc_start[block]
        queries = lax.dynamic_index_in_dim(query_set, index, 0, False).reshape(
            BLK, kv_heads, group, HD
        )

        def per_tile(tile, carry):
            running, total, accum = carry
            keys = lax.dynamic_index_in_dim(keys_all, tile - first_block, 0, False).reshape(
                BLK, kv_heads, HD
            )
            values = lax.dynamic_index_in_dim(values_all, tile - first_block, 0, False).reshape(
                BLK, kv_heads, HD
            )
            scores = (
                jnp.einsum("qkgd,skd->kgqs", queries, keys, preferred_element_type=jnp.float32)
                * scale
            )
            allowed = causal | (tile < block)
            scores = jnp.where(allowed, scores, -jnp.inf)
            highest = jnp.maximum(running, jnp.max(scores, axis=3))
            factor = jnp.exp(running - highest)
            expo = jnp.exp(scores - highest[..., None])
            total = total * factor + jnp.sum(expo, axis=3)
            accum = accum * factor[..., None] + jnp.einsum(
                "kgqs,skd->kgqd",
                expo.astype(jnp.bfloat16),
                values,
                preferred_element_type=jnp.float32,
            )
            return (highest, total, accum)

        start_state = (
            jnp.full((kv_heads, group, BLK), -jnp.inf, jnp.float32),
            jnp.zeros((kv_heads, group, BLK), jnp.float32),
            jnp.zeros((kv_heads, group, BLK, HD), jnp.float32),
        )
        _, total, accum = lax.fori_loop(begin, block + 1, per_tile, start_state)
        mixed = (
            (accum / total[..., None])
            .transpose(2, 0, 1, 3)
            .reshape(BLK, q_width)
            .astype(jnp.bfloat16)
        )
        return lax.dynamic_update_index_in_dim(result, mixed, index, 0)

    return lax.fori_loop(0, count, per_block, jnp.zeros((count, BLK, q_width), jnp.bfloat16))


def shards(query, key, value, doc_ids, plan):
    head_count = lax.axis_size("head")
    shard_count = lax.axis_size("ctx")
    local_rows = query.shape[0]
    q_parts = query.reshape(local_rows, head_count, query.shape[1] // head_count)
    k_parts = key.reshape(local_rows, head_count, key.shape[1] // head_count)
    v_parts = value.reshape(local_rows, head_count, value.shape[1] // head_count)
    q_heads, k_heads, v_heads = (
        lax.all_to_all(q_parts, "head", split_axis=1, concat_axis=0, tiled=True),
        lax.all_to_all(k_parts, "head", split_axis=1, concat_axis=0, tiled=True),
        lax.all_to_all(v_parts, "head", split_axis=1, concat_axis=0, tiled=True),
    )
    blocks_here = head_count * local_rows // BLK
    q_width = q_heads.shape[2]
    kv_width = k_heads.shape[2]
    kv_heads = kv_width // HD
    group = q_width // HD // kv_heads
    q_blocks = q_heads.reshape(blocks_here, BLK, q_width)
    k_blocks = k_heads.reshape(blocks_here, BLK, kv_width)
    v_blocks = v_heads.reshape(blocks_here, BLK, kv_width)
    shard = lax.axis_index("ctx")
    total_blocks = doc_ids.shape[0]
    block_iota = jnp.arange(total_blocks, dtype=jnp.int32)
    doc_start = jnp.sum((doc_ids[None, :] < doc_ids[:, None]).astype(jnp.int32), axis=1)
    position = jnp.zeros((total_blocks,), jnp.int32).at[plan].set(block_iota)
    target = position // blocks_here
    target_grid = target.reshape(shard_count, blocks_here)
    local_iota = jnp.arange(blocks_here, dtype=jnp.int32)
    lower = local_iota[None, :] < local_iota[:, None]
    same_before = (target_grid[:, :, None] == target_grid[:, None, :]) & lower[None, :, :]
    rank = jnp.sum(same_before.astype(jnp.int32), axis=2).reshape(total_blocks)
    capacity = -(-blocks_here // shard_count)
    slots = shard_count * capacity
    slot_iota = jnp.arange(slots, dtype=jnp.int32)
    own_ids = shard * blocks_here + local_iota
    plan_ids = lax.dynamic_slice_in_dim(plan, shard * blocks_here, blocks_here)
    depth = (MAXDOC - 2 + blocks_here) // blocks_here
    stacked = jnp.stack([k_blocks, v_blocks])
    pieces = []
    pieces.append(shifted(stacked, "ctx", 1))
    pieces.append(stacked)
    window = jnp.concatenate(pieces, axis=1)
    local_out = attend(
        q_blocks,
        own_ids,
        window[0],
        window[1],
        (shard - depth) * blocks_here,
        doc_start,
        kv_heads,
        group,
    )
    slot = target[own_ids] * capacity + rank[own_ids]
    select = (slot_iota[:, None] == slot[None, :]).astype(jnp.bfloat16)
    flat = local_out.reshape(blocks_here, BLK * q_width)
    received = lax.all_to_all(
        jnp.dot(select, flat, preferred_element_type=jnp.bfloat16).reshape(slots, BLK, q_width),
        "ctx",
        split_axis=0,
        concat_axis=0,
        tiled=True,
    )
    slot = plan_ids // blocks_here * capacity + rank[plan_ids]
    select = (slot[:, None] == slot_iota[None, :]).astype(jnp.bfloat16)
    flat = received.reshape(slots, BLK * q_width)
    result = jnp.dot(select, flat, preferred_element_type=jnp.bfloat16).reshape(
        blocks_here, BLK, q_width
    )
    return result.reshape(blocks_here * BLK, q_width)


def solution(mesh):
    return jax.shard_map(
        shards,
        mesh=mesh,
        in_specs=(
            P(("ctx", "head"), None),
            P(("ctx", "head"), None),
            P(("ctx", "head"), None),
            P(),
            P(),
        ),
        out_specs=P("ctx", "head"),
        check_vma=False,
    )
```

profile of v0, /device:TPU:0, one launch (start us, length us, event | category | flops | bytes accessed | tf_op | source)
XLA Modules:
  0.0 840.9 jit_solution(10675207682483674420)
XLA Ops:
  2.3 4.3 all-to-all-start.1
  8.8 12.2 %all-to-all-done.1 = bf16[512,4,256]{0,2,1:T(8,128)(2,1)S(1)} async-done(((bf16[512,4,256]{0,2,1:T(8,128)(2,1)}), bf16[512,4,256]{0,2,1:T(8,128)(2,1)S(1)}, u32[]{:S(2)}, u32[]{:S(2)}) %all-to-all-start.1) | async-done | bytes 1048608 | tf_op jit(solution)/shard_map/all_to_all | solution.py:85
  24.5 12.0 %copy.65 = bf16[512,8192]{0,1:T(8,128)(2,1)} copy(bf16[512,8192]{1,0:T(8,128)(2,1)} %param.9) | data formatting | bytes 16777216 | tf_op args[0]
  38.9 5.7 all-to-all-start
  47.2 5.4 collective-permute-start
  55.6 41.5 %collective-permute-done = bf16[2,16,128,256]{3,2,1,0:T(8,128)(2,1)} collective-permute-done((bf16[2,16,128,256]{3,2,1,0:T(8,128)(2,1)}, bf16[2,16,128,256]{3,2,1,0:T(8,128)(2,1)}, u32[]{:S(2)}, u32[]{:S(2)}) %collective-permute-start) | collective-permute-done | bytes 2097184 | tf_op jit(solution)/shard_map/ppermute | solution.py:16
  107.4 30.2 %all-to-all-done = bf16[512,4,2048]{0,2,1:T(8,128)(2,1)} async-done(((bf16[512,4,2048]{0,2,1:T(8,128)(2,1)}), bf16[512,4,2048]{0,2,1:T(8,128)(2,1)}, u32[]{:S(2)}, u32[]{:S(2)}) %all-to-all-start) | async-done | bytes 8388640 | tf_op jit(solution)/shard_map/all_to_all | solution.py:84
  137.7 11.5 %copy.66 = bf16[4,512,1,2048]{3,1,0,2:T(8,128)(2,1)} copy(bf16[4,512,1,2048]{1,3,0,2:T(8,128)(2,1)} %bitcast.9) | data formatting | bytes 16777216 | tf_op jit(solution)/shard_map/all_to_all | solution.py:84
  149.2 447.3 %while.46 = (s32[]{:T(128)}, bf16[16,128,2048]{2,1,0:T(8,128)(2,1)}, s32[16]{0:T(128)S(1)}, s32[128]{0:T(128)S(1)}, bf16[16,128,2048]{2,1,0:T(8,128)(2,1)}, /*in...) while((s32[]{:T(128)}, ...), condition=%wide.region_8.9_spmd.clone, body=%wide.region_3.8_spmd.clone.sunk | while | flops 137138176 | bytes 15295024 | solution.py:73
  154.4 5.2 while.47
  166.5 9.7 %while.47 = (s32[]{:T(128)}, f32[2,8,128]{2,1,0:T(8,128)S(1)}, f32[2,8,128]{2,1,0:T(8,128)S(1)}, f32[2,8,128,128]{3,2,1,0:T(8,128)S(1)}, s32[]{:T(128)}, /*index...) while((s32[]{:T(128)}, f32[2,8,128]{2,1,0:T(8,128)S(1)}, ...), condition=%wide.region_7.7_spmd, body=%wide.region_4.6_spmd.sunk | while | flops 136597504 | bytes 6340809 | solution.py:64
  183.1 14.2 %while.47 = (s32[]{:T(128)}, f32[2,8,128]{2,1,0:T(8,128)S(1)}, f32[2,8,128]{2,1,0:T(8,128)S(1)}, f32[2,8,128,128]{3,2,1,0:T(8,128)S(1)}, s32[]{:T(128)}, /*index...) while((s32[]{:T(128)}, f32[2,8,128]{2,1,0:T(8,128)S(1)}, ...), condition=%wide.region_7.7_spmd, body=%wide.region_4.6_spmd.sunk | while | flops 136597504 | bytes 6340809 | solution.py:64
  204.3 18.7 %while.47 = (s32[]{:T(128)}, f32[2,8,128]{2,1,0:T(8,128)S(1)}, f32[2,8,128]{2,1,0:T(8,128)S(1)}, f32[2,8,128,128]{3,2,1,0:T(8,128)S(1)}, s32[]{:T(128)}, /*index...) while((s32[]{:T(128)}, f32[2,8,128]{2,1,0:T(8,128)S(1)}, ...), condition=%wide.region_7.7_spmd, body=%wide.region_4.6_spmd.sunk | while | flops 136597504 | bytes 6340809 | solution.py:64
  230.0 23.3 %while.47 = (s32[]{:T(128)}, f32[2,8,128]{2,1,0:T(8,128)S(1)}, f32[2,8,128]{2,1,0:T(8,128)S(1)}, f32[2,8,128,128]{3,2,1,0:T(8,128)S(1)}, s32[]{:T(128)}, /*index...) while((s32[]{:T(128)}, f32[2,8,128]{2,1,0:T(8,128)S(1)}, ...), condition=%wide.region_7.7_spmd, body=%wide.region_4.6_spmd.sunk | while | flops 136597504 | bytes 6340809 | solution.py:64
  260.2 27.8 %while.47 = (s32[]{:T(128)}, f32[2,8,128]{2,1,0:T(8,128)S(1)}, f32[2,8,128]{2,1,0:T(8,128)S(1)}, f32[2,8,128,128]{3,2,1,0:T(8,128)S(1)}, s32[]{:T(128)}, /*index...) while((s32[]{:T(128)}, f32[2,8,128]{2,1,0:T(8,128)S(1)}, ...), condition=%wide.region_7.7_spmd, body=%wide.region_4.6_spmd.sunk | while | flops 136597504 | bytes 6340809 | solution.py:64
  294.9 32.3 %while.47 = (s32[]{:T(128)}, f32[2,8,128]{2,1,0:T(8,128)S(1)}, f32[2,8,128]{2,1,0:T(8,128)S(1)}, f32[2,8,128,128]{3,2,1,0:T(8,128)S(1)}, s32[]{:T(128)}, /*index...) while((s32[]{:T(128)}, f32[2,8,128]{2,1,0:T(8,128)S(1)}, ...), condition=%wide.region_7.7_spmd, body=%wide.region_4.6_spmd.sunk | while | flops 136597504 | bytes 6340809 | solution.py:64
  334.2 36.8 %while.47 = (s32[]{:T(128)}, f32[2,8,128]{2,1,0:T(8,128)S(1)}, f32[2,8,128]{2,1,0:T(8,128)S(1)}, f32[2,8,128,128]{3,2,1,0:T(8,128)S(1)}, s32[]{:T(128)}, /*index...) while((s32[]{:T(128)}, f32[2,8,128]{2,1,0:T(8,128)S(1)}, ...), condition=%wide.region_7.7_spmd, body=%wide.region_4.6_spmd.sunk | while | flops 136597504 | bytes 6340809 | solution.py:64
  378.0 5.2 while.47
  390.1 9.7 %while.47 = (s32[]{:T(128)}, f32[2,8,128]{2,1,0:T(8,128)S(1)}, f32[2,8,128]{2,1,0:T(8,128)S(1)}, f32[2,8,128,128]{3,2,1,0:T(8,128)S(1)}, s32[]{:T(128)}, /*index...) while((s32[]{:T(128)}, f32[2,8,128]{2,1,0:T(8,128)S(1)}, ...), condition=%wide.region_7.7_spmd, body=%wide.region_4.6_spmd.sunk | while | flops 136597504 | bytes 6340809 | solution.py:64
  406.8 14.2 %while.47 = (s32[]{:T(128)}, f32[2,8,128]{2,1,0:T(8,128)S(1)}, f32[2,8,128]{2,1,0:T(8,128)S(1)}, f32[2,8,128,128]{3,2,1,0:T(8,128)S(1)}, s32[]{:T(128)}, /*index...) while((s32[]{:T(128)}, f32[2,8,128]{2,1,0:T(8,128)S(1)}, ...), condition=%wide.region_7.7_spmd, body=%wide.region_4.6_spmd.sunk | while | flops 136597504 | bytes 6340809 | solution.py:64
  427.9 18.7 %while.47 = (s32[]{:T(128)}, f32[2,8,128]{2,1,0:T(8,128)S(1)}, f32[2,8,128]{2,1,0:T(8,128)S(1)}, f32[2,8,128,128]{3,2,1,0:T(8,128)S(1)}, s32[]{:T(128)}, /*index...) while((s32[]{:T(128)}, f32[2,8,128]{2,1,0:T(8,128)S(1)}, ...), condition=%wide.region_7.7_spmd, body=%wide.region_4.6_spmd.sunk | while | flops 136597504 | bytes 6340809 | solution.py:64
  453.6 23.3 %while.47 = (s32[]{:T(128)}, f32[2,8,128]{2,1,0:T(8,128)S(1)}, f32[2,8,128]{2,1,0:T(8,128)S(1)}, f32[2,8,128,128]{3,2,1,0:T(8,128)S(1)}, s32[]{:T(128)}, /*index...) while((s32[]{:T(128)}, f32[2,8,128]{2,1,0:T(8,128)S(1)}, ...), condition=%wide.region_7.7_spmd, body=%wide.region_4.6_spmd.sunk | while | flops 136597504 | bytes 6340809 | solution.py:64
  483.8 27.8 %while.47 = (s32[]{:T(128)}, f32[2,8,128]{2,1,0:T(8,128)S(1)}, f32[2,8,128]{2,1,0:T(8,128)S(1)}, f32[2,8,128,128]{3,2,1,0:T(8,128)S(1)}, s32[]{:T(128)}, /*index...) while((s32[]{:T(128)}, f32[2,8,128]{2,1,0:T(8,128)S(1)}, ...), condition=%wide.region_7.7_spmd, body=%wide.region_4.6_spmd.sunk | while | flops 136597504 | bytes 6340809 | solution.py:64
  518.6 32.3 %while.47 = (s32[]{:T(128)}, f32[2,8,128]{2,1,0:T(8,128)S(1)}, f32[2,8,128]{2,1,0:T(8,128)S(1)}, f32[2,8,128,128]{3,2,1,0:T(8,128)S(1)}, s32[]{:T(128)}, /*index...) while((s32[]{:T(128)}, f32[2,8,128]{2,1,0:T(8,128)S(1)}, ...), condition=%wide.region_7.7_spmd, body=%wide.region_4.6_spmd.sunk | while | flops 136597504 | bytes 6340809 | solution.py:64
  557.8 36.8 %while.47 = (s32[]{:T(128)}, f32[2,8,128]{2,1,0:T(8,128)S(1)}, f32[2,8,128]{2,1,0:T(8,128)S(1)}, f32[2,8,128,128]{3,2,1,0:T(8,128)S(1)}, s32[]{:T(128)}, /*index...) while((s32[]{:T(128)}, f32[2,8,128]{2,1,0:T(8,128)S(1)}, ...), condition=%wide.region_7.7_spmd, body=%wide.region_4.6_spmd.sunk | while | flops 136597504 | bytes 6340809 | solution.py:64
  596.4 16.1 %fusion.9 = bf16[16,128,2048]{2,0,1:T(8,128)(2,1)} fusion(s32[16]{0:T(128)S(1)} %multiply_add_fusion.1, bf16[2,8,128,2048]{3,2,1,0:T(8,128)(2,1)} %bitcast.91), kind=kOutput, calls=%fused_computation.23 | convolution fusion | flops 134217984 | bytes 16777280 | tf_op jit(solution)/shard_map/dot_general | solution.py:132
  612.6 11.6 %copy.75 = bf16[16,128,2048]{2,1,0:T(8,128)(2,1)} copy(bf16[16,128,2048]{2,0,1:T(8,128)(2,1)} %fusion.9) | data formatting | bytes 16777216 | tf_op jit(solution)/shard_map/dot_general | solution.py:132
  624.2 5.5 all-to-all-start.3
  630.5 182.0 %all-to-all-done.3 = bf16[16,128,2048]{2,1,0:T(8,128)(2,1)} async-done(((bf16[16,128,2048]{2,1,0:T(8,128)(2,1)}), bf16[16,128,2048]{2,1,0:T(8,128)(2,1)}, u32[]{:S(2)}, u32[]{:S(2)}) %all-to-all-start.3) | async-done | bytes 8388640 | tf_op jit(solution)/shard_map/all_to_all | solution.py:131
  812.5 11.4 %copy.86 = bf16[2,8,128,2048]{3,1,2,0:T(8,128)(2,1)} copy(bf16[2,8,128,2048]{3,2,1,0:T(8,128)(2,1)} %bitcast.40) | data formatting | bytes 16777216
  824.0 9.0 %fusion.12 = bf16[16,262144]{1,0:T(8,128)(2,1)} fusion(bf16[16,262144]{1,0:T(8,128)(2,1)} %bitcast.84, s32[16]{0:T(128)S(1)} %multiply_add_fusion.2), kind=kOutput, calls=%fused_computation.35 | convolution fusion | flops 134217984 | bytes 16777280 | tf_op jit(solution)/shard_map/dot_general | solution.py:141
  832.9 8.0 reshape_reshape.3
  (819 shorter events, 254.3 us)
Async XLA Ops:
  2.3 18.7 %all-to-all-start.1 = ((bf16[512,4,256]{0,2,1:T(8,128)(2,1)}), bf16[512,4,256]{0,2,1:T(8,128)(2,1)S(1)}, u32[]{:S(2)}, u32[]{:S(2)}) async-start(bf16[512,4,256]{0,2,1:T(8,128)(2,1)} %bitcast.11), calls=%async_computation.1 | async-start | bytes 2097152 | tf_op jit(solution)/shard_map/all_to_all | solution.py:85
  21.0 17.9 %all-to-all-start.2 = ((bf16[512,4,256]{0,2,1:T(8,128)(2,1)}), bf16[512,4,256]{0,2,1:T(8,128)(2,1)S(1)}, u32[]{:S(2)}, u32[]{:S(2)}) async-start(bf16[512,4,256]{0,2,1:T(8,128)(2,1)} %bitcast.15), calls=%async_computation.2 | async-start | bytes 2097152 | tf_op jit(solution)/shard_map/all_to_all | solution.py:86
  38.9 98.8 %all-to-all-start = ((bf16[512,4,2048]{0,2,1:T(8,128)(2,1)}), bf16[512,4,2048]{0,2,1:T(8,128)(2,1)}, u32[]{:S(2)}, u32[]{:S(2)}) async-start(bf16[512,4,2048]{0,2,1:T(8,128)(2,1)} %bitcast.85), calls=%async_computation | async-start | bytes 16777216 | tf_op jit(solution)/shard_map/all_to_all | solution.py:84
  44.5 8.0 copy-start
  44.6 10.8 %copy-start.1 = (s32[128]{0:T(128)S(1)}, s32[128]{0:T(128)}, u32[]{:S(2)}) copy-start(s32[128]{0:T(128)} %param.12) | copy-start | bytes 1540
  47.2 49.9 %collective-permute-start = (bf16[2,16,128,256]{3,2,1,0:T(8,128)(2,1)}, bf16[2,16,128,256]{3,2,1,0:T(8,128)(2,1)}, u32[]{:S(2)}, u32[]{:S(2)}) collective-permute-start(bf16[2,16,128,256]{3,2,1,0:T(8,128)(2,1)} %pad_maximum_fusion), channel_id=1, source_target_pairs={{0,4},{4,8},{8,12},{12,16},{16,20},{20,24},{24,28},{1,5},{5,9},{9,... | collective-permute-start | bytes 6291464 | tf_op jit(solution)/shard_map/ppermute | solution.py:16
  624.2 188.4 %all-to-all-start.3 = ((bf16[16,128,2048]{2,1,0:T(8,128)(2,1)}), bf16[16,128,2048]{2,1,0:T(8,128)(2,1)}, u32[]{:S(2)}, u32[]{:S(2)}) async-start(bf16[16,128,2048]{2,1,0:T(8,128)(2,1)} %copy.75), calls=%async_computation.3 | async-start | bytes 16777216 | tf_op jit(solution)/shard_map/all_to_all | solution.py:131
where the time goes:
time: 849 us; the launch traced here: 841 us
  waiting for transfers between devices  268 us (32%)
  loops' own time  220 us (26%)
  local copies, waits for them, and re-layouts  205 us (24%)
  matrix products  99.2 us (12%)
  starting transfers between devices  24.3 us (3%)
  other arithmetic  23.3 us (3%)
    another operation x16, loops' own time, per_block(): _, total, accum = lax.fori_loop(begin, block + 1, per_tile, start_state)  184 us
    all_to_all x1, waiting for transfers between devices, shards(): lax.all_to_all(jnp.dot(select, flat, preferred_element_type=jnp.bfloat16)...  182 us
    dynamic_slice x72, local copies, waits for them, and re-layouts, per_tile(): lax.dynamic_index_in_dim(values_all, tile - first_block, 0, False)  64 us
    dot_general x72, matrix products, per_tile(): jnp.einsum('kgqs,skd->kgqd', expo.astype(jnp.bfloat16), values, preferred...  48.2 us
    ppermute x1, waiting for transfers between devices, shifted(): return lax.ppermute(shard, axis, pairs)  41.5 us
    another operation x1, loops' own time, attend(): lax.fori_loop(0, count, per_block, jnp.zeros((count, BLK, q_width), jnp.b...  36.1 us
    unnamed x10, local copies, waits for them, and re-layouts  34.9 us
    all_to_all x1, waiting for transfers between devices, shards(): lax.all_to_all(q_parts, 'head', split_axis=1, concat_axis=0, tiled=True)  30.2 us
  transfers between devices with their start and end apart: 5, of which 5 were waited for; matrix products, arithmetic and copies ran while one was open for 4% of the time, Pallas kernels for 0%

commit v1 on v0

v1 whole, which is shorter than its diff:
```python
import functools
import math

import jax
import jax.numpy as jnp
from jax import lax
from jax.experimental import pallas as pl
from jax.experimental.pallas import tpu as pltpu
from jax.sharding import PartitionSpec as P

HD = 128
BLK = 128
MAXDOC = 8
CHUNKS = 4
ROW_HEADS = 2


def attend_kernel(heads, block_ref, count_ref, q_ref, k_ref, v_ref, o_ref):
    slot = pl.program_id(0)
    block = block_ref[slot]
    count = count_ref[slot]
    factor = math.log2(math.e) / math.sqrt(HD)
    rows = ROW_HEADS * BLK
    row_pos = lax.rem(lax.broadcasted_iota(jnp.int32, (rows, BLK), 0), BLK)
    causal = lax.broadcasted_iota(jnp.int32, (rows, BLK), 1) <= row_pos

    def body(pairs):
        width = 2 * pairs * BLK
        first = pl.multiple_of((block + MAXDOC - 2 * pairs) * BLK, BLK)
        keys = k_ref[pl.ds(first, width), :]
        values = v_ref[pl.ds(first, width), :]
        inside = jnp.full((rows, BLK), count - (2 * pairs - 1), jnp.int32) > 0
        for step in range(heads // ROW_HEADS):
            base = step * ROW_HEADS * HD
            queries = jnp.concatenate(
                [q_ref[:, base + i * HD : base + (i + 1) * HD] for i in range(ROW_HEADS)], axis=0
            )
            scores = lax.dot_general(
                queries, keys, (((1,), (1,)), ((), ())), preferred_element_type=jnp.float32
            )
            parts = [scores[:, i * BLK : (i + 1) * BLK] for i in range(2 * pairs)]
            parts[0] = jnp.where(inside, parts[0], -jnp.inf)
            parts[-1] = jnp.where(causal, parts[-1], -jnp.inf)
            top = functools.reduce(jnp.maximum, parts)
            top = jnp.max(top, axis=1, keepdims=True)
            parts = [jnp.exp2((part - top) * factor) for part in parts]
            total = jnp.sum(functools.reduce(jnp.add, parts), axis=1, keepdims=True)
            weights = jnp.concatenate([part.astype(jnp.bfloat16) for part in parts], axis=1)
            mixed = jnp.dot(weights, values, preferred_element_type=jnp.float32) / total
            mixed = mixed.astype(o_ref.dtype)
            for i in range(ROW_HEADS):
                o_ref[0, :, base + i * HD : base + (i + 1) * HD] = mixed[i * BLK : (i + 1) * BLK]

    for pairs in range(1, MAXDOC // 2 + 1):

        @pl.when((count + 1) // 2 == pairs)
        def _():
            body(pairs)


def attend(slot_block, slot_count, queries, keys, values, kv_head):
    slots = slot_block.shape[0]
    width = queries.shape[1]
    heads = width // HD
    window = keys.shape[0]
    flops = 4 * slots * heads * BLK * BLK * HD * 5
    return pl.pallas_call(
        functools.partial(attend_kernel, heads),
        out_shape=jax.ShapeDtypeStruct((slots, BLK, width), jnp.bfloat16),
        grid_spec=pltpu.PrefetchScalarGridSpec(
            num_scalar_prefetch=2,
            grid=(slots,),
            in_specs=[
                pl.BlockSpec((BLK, width), lambda s, b, n: (b[s], 0)),
                pl.BlockSpec((window, HD), lambda s, b, n: (0, kv_head)),
                pl.BlockSpec((window, HD), lambda s, b, n: (0, kv_head)),
            ],
            out_specs=pl.BlockSpec((1, BLK, width), lambda s, b, n: (s, 0, 0)),
        ),
        compiler_params=pltpu.CompilerParams(dimension_semantics=("arbitrary",)),
        cost_estimate=pl.CostEstimate(
            flops=flops, transcendentals=0, bytes_accessed=4 * queries.size + 4 * keys.size
        ),
        name="attend",
    )(slot_block, slot_count, queries, keys, values)


def place_kernel(slot_ref, x_ref, *rest):
    rest[-1][...] = x_ref[0]


def place(slot_of, received, so_far, chunk, chunks):
    blocks = slot_of.shape[0]
    width = received.shape[2]
    in_specs = [pl.BlockSpec((1, BLK, width), lambda i, s: (s[i], 0, 0))]
    operands = [slot_of, received]
    aliases = {}
    if so_far is not None:
        in_specs.append(pl.BlockSpec(memory_space=pl.ANY))
        operands.append(so_far)
        aliases = {2: 0}
    return pl.pallas_call(
        place_kernel,
        out_shape=jax.ShapeDtypeStruct((blocks * BLK, width * chunks), jnp.bfloat16),
        grid_spec=pltpu.PrefetchScalarGridSpec(
            num_scalar_prefetch=1,
            grid=(blocks,),
            in_specs=in_specs,
            out_specs=pl.BlockSpec((BLK, width), lambda i, s: (i, chunk)),
        ),
        compiler_params=pltpu.CompilerParams(dimension_semantics=("arbitrary",)),
        cost_estimate=pl.CostEstimate(
            flops=0, transcendentals=0, bytes_accessed=4 * blocks * BLK * width
        ),
        input_output_aliases=aliases,
        name="place",
    )(*operands)


def shifted(shard, axis, by):
    count = lax.axis_size(axis)
    pairs = [(i, i + by) for i in range(count) if 0 <= i + by < count]
    return lax.ppermute(shard, axis, pairs)


def shards(query, key, value, doc_ids, plan):
    head_count = lax.axis_size("head")
    shard_count = lax.axis_size("ctx")
    local_rows = query.shape[0]
    rows = head_count * local_rows
    blocks_here = rows // BLK
    q_width = query.shape[1] // head_count
    kv_width = key.shape[1] // head_count
    kv_heads = kv_width // HD
    width = q_width // CHUNKS
    per_kv = CHUNKS // kv_heads

    def exchange(parts):
        return lax.all_to_all(parts, "head", split_axis=0, concat_axis=0, tiled=True)

    kv = jnp.stack(
        [
            jnp.stack([x[:, h * kv_width : (h + 1) * kv_width] for x in (key, value)])
            for h in range(head_count)
        ]
    )
    kv = exchange(kv)
    kv = kv.transpose(1, 0, 2, 3).reshape(2, rows, kv_width)
    before = shifted(kv[:, rows - (MAXDOC - 1) * BLK :], "ctx", 1)

    shard = lax.axis_index("ctx")
    doc_start = jnp.sum((doc_ids[None, :] < doc_ids[:, None]).astype(jnp.int32), axis=1)
    counts = jnp.arange(doc_ids.shape[0], dtype=jnp.int32) - doc_start + 1
    own_counts = lax.dynamic_slice_in_dim(counts, shard * blocks_here, blocks_here)
    capacity = -(-blocks_here // shard_count)
    slots = shard_count * capacity
    grid = plan.reshape(shard_count, blocks_here)
    source = grid // blocks_here
    local = grid % blocks_here
    iota = jnp.arange(blocks_here, dtype=jnp.int32)
    lower = (iota[None, :] < iota[:, None])[None]
    rank = jnp.sum(
        ((source[:, :, None] == source[:, None, :]) & lower).astype(jnp.int32), axis=2
    )
    hit = (source == shard)[:, None, :] & (
        rank[:, None, :] == jnp.arange(capacity, dtype=jnp.int32)[None, :, None]
    )
    hit = hit.reshape(slots, blocks_here)
    local = jnp.broadcast_to(local[:, None, :], (shard_count, capacity, blocks_here))
    local = local.reshape(slots, blocks_here)
    slot_block = jnp.sum(jnp.where(hit, local, 0), axis=1)
    one_hot = hit[:, :, None] & (local[:, :, None] == iota[None, None, :])
    slot_count = jnp.sum(jnp.where(one_hot, own_counts[None, None, :], 0), axis=(1, 2))
    mine = lax.dynamic_index_in_dim(source * capacity + rank, shard, 0, False)

    window_k = jnp.concatenate([before[0], kv[0]], axis=0)
    window_v = jnp.concatenate([before[1], kv[1]], axis=0)

    result = None
    for chunk in range(CHUNKS):
        q = jnp.stack(
            [
                query[:, h * q_width + chunk * width : h * q_width + (chunk + 1) * width]
                for h in range(head_count)
            ]
        )
        q = exchange(q).reshape(rows, width)
        out = attend(slot_block, slot_count, q, window_k, window_v, chunk // per_kv)
        received = lax.all_to_all(out, "ctx", split_axis=0, concat_axis=0, tiled=True)
        result = place(mine, received, result, chunk, CHUNKS)
    return result


def solution(mesh):
    return jax.shard_map(
        shards,
        mesh=mesh,
        in_specs=(
            P(("ctx", "head"), None),
            P(("ctx", "head"), None),
            P(("ctx", "head"), None),
            P(),
            P(),
        ),
        out_specs=P("ctx", "head"),
        check_vma=False,
    )
```

time: 849 us -> 381 us (0.45)
  loops' own time: 220 us -> 0 us
  local copies, waits for them, and re-layouts: 205 us -> 14.3 us
  Pallas kernels: 0 us -> 111 us
  matrix products: 99.2 us -> 0 us
  waiting for transfers between devices: 268 us -> 191 us
  starting transfers between devices: 24.3 us -> 46.3 us
    another operation x17 -> x0, loops' own time: 220 us -> none  [the longest x16 184 us: per_block(): _, total, accum = lax.fori_loop(begin, block + 1, per_tile, start_state)]
    pallas_call x0 -> x8, Pallas kernels: none -> 111 us  [the longest x4 70.5 us: attend(): pl.pallas_call(functools.partial(attend_kernel, heads), out_shape=jax.Sha...]
    dynamic_slice x136 -> x1, local copies, waits for them, and re-layouts: 104 us -> 0.08 us  [shards(): lax.dynamic_slice_in_dim(counts, shard * blocks_here, blocks_here)]
    dot_general x146 -> x0, matrix products: 99.2 us -> none  [the longest x72 48.2 us: per_tile(): jnp.einsum('kgqs,skd->kgqd', expo.astype(jnp.bfloat16), values, preferred...]
    ppermute x1, waiting for transfers between devices: 41.5 us -> 0.01 us  [shifted(): return lax.ppermute(shard, axis, pairs)]
    all_to_all x4 -> x9, waiting for transfers between devices: 227 us -> 191 us  [the longest x4 108 us: shards(): lax.all_to_all(out, 'ctx', split_axis=0, concat_axis=0, tiled=True)]
    unnamed x10 -> x14, local copies, waits for them, and re-layouts: 34.9 us -> 2.9 us
    all_to_all x4 -> x9, starting transfers between devices: 18.9 us -> 41.2 us  [the longest x5 22.1 us: exchange(): lax.all_to_all(parts, 'head', split_axis=0, concat_axis=0, tiled=True)]
  transfers between devices with their start and end apart: 5 -> 10, of which waited for: 5 -> 9; matrix products, arithmetic and copies ran while one was open for 4% -> 6% of each run, Pallas kernels for 0% -> 27%
where the time goes in v1:
time: 381 us; the launch traced here: 378 us
  waiting for transfers between devices  191 us (50%)
  Pallas kernels  111 us (29%)
  starting transfers between devices  46.3 us (12%)
  other arithmetic  15.4 us (4%)
  local copies, waits for them, and re-layouts  14.3 us (4%)
    all_to_all x4, waiting for transfers between devices, shards(): lax.all_to_all(out, 'ctx', split_axis=0, concat_axis=0, tiled=True)  108 us
    all_to_all x5, waiting for transfers between devices, exchange(): lax.all_to_all(parts, 'head', split_axis=0, concat_axis=0, tiled=True)  82.7 us
    pallas_call x4, Pallas kernels, attend(): pl.pallas_call(functools.partial(attend_kernel, heads), out_shape=jax.Sha...  70.5 us
    pallas_call x4, Pallas kernels, place(): pl.pallas_call(place_kernel, out_shape=jax.ShapeDtypeStruct((blocks * BLK...  40.6 us
    all_to_all x5, starting transfers between devices, exchange(): lax.all_to_all(parts, 'head', split_axis=0, concat_axis=0, tiled=True)  22.1 us
    all_to_all x4, starting transfers between devices, shards(): lax.all_to_all(out, 'ctx', split_axis=0, concat_axis=0, tiled=True)  19.1 us
    another operation x4, other arithmetic, shards(): jnp.stack([query[:, h * q_width + chunk * width:h * q_width + (chunk + 1)...  9.38 us
  transfers between devices with their start and end apart: 10, of which 9 were waited for; matrix products, arithmetic and copies ran while one was open for 6% of the time, Pallas kernels for 27%

profile of v1, /device:TPU:0, one launch (start us, length us, event | category | flops | bytes accessed | tf_op | source)
XLA Modules:
  0.0 377.9 jit_solution(1115280652915088425)
XLA Ops:
  1.8 1.6 pad_maximum_fusion.1
  3.4 4.3 %all-to-all-start.1 = ((bf16[4,2,512,256]{3,2,1,0:T(8,128)(2,1)}), bf16[4,2,512,256]{3,2,1,0:T(8,128)(2,1)S(1)}, u32[]{:S(2)}, u32[]{:S(2)}) async-start(bf16[4,2,512,256]{3,2,1,0:T(8,128)(2,1)} %pad_maximum_fusion.1), calls=%async_computation.1 | async-start | bytes 4194304 | tf_op jit(solution)/shard_map/all_to_all | solution.py:139
  7.7 5.9 %slice_bitcast_fusion.3 = (bf16[1,512,512]{2,1,0:T(8,128)(2,1)S(1)}, bf16[1,512,512]{2,1,0:T(8,128)(2,1)S(1)}, bf16[1,512,512]{2,1,0:T(8,128)(2,1)}, bf16[1,512,...) fusion(bf16[512,8192]{1,0:T(8,128)(2,1)} %param.5), kind=kLoop, calls=%fused_computation.14 | loop fusion | bytes 16777216 | tf_op jit(solution)/shard_map/stack | solution.py:181
  15.2 18.2 %all-to-all-done.1 = bf16[4,2,512,256]{3,2,1,0:T(8,128)(2,1)S(1)} async-done(((bf16[4,2,512,256]{3,2,1,0:T(8,128)(2,1)}), bf16[4,2,512,256]{3,2,1,0:T(8,128)(2,1)S(1)}, u32[]{:S(2)}, u32[]{:S(2)}) %all-to-all-start.1) | async-done | bytes 2097184 | tf_op jit(solution)/shard_map/all_to_all | solution.py:139
  33.4 4.5 %all-to-all-start.7 = ((bf16[4,512,512]{2,1,0:T(8,128)(2,1)}), bf16[4,512,512]{2,1,0:T(8,128)(2,1)}, u32[]{:S(2)}, u32[]{:S(2)}) async-start(bf16[4,512,512]{2,1,0:T(8,128)(2,1)} %pad_maximum_fusion.4), calls=%async_computation.7 | async-start | bytes 4194304 | tf_op jit(solution)/shard_map/all_to_all | solution.py:139
  37.8 3.1 pad_maximum_fusion.3
  40.9 22.6 %all-to-all-done.7 = bf16[4,512,512]{2,1,0:T(8,128)(2,1)} async-done(((bf16[4,512,512]{2,1,0:T(8,128)(2,1)}), bf16[4,512,512]{2,1,0:T(8,128)(2,1)}, u32[]{:S(2)}, u32[]{:S(2)}) %all-to-all-start.7) | async-done | bytes 2097184 | tf_op jit(solution)/shard_map/all_to_all | solution.py:139
  63.5 4.4 %all-to-all-start.5 = ((bf16[4,512,512]{2,1,0:T(8,128)(2,1)}), bf16[4,512,512]{2,1,0:T(8,128)(2,1)}, u32[]{:S(2)}, u32[]{:S(2)}) async-start(bf16[4,512,512]{2,1,0:T(8,128)(2,1)} %pad_maximum_fusion.3), calls=%async_computation.5 | async-start | bytes 4194304 | tf_op jit(solution)/shard_map/all_to_all | solution.py:139
  68.0 3.1 pad_maximum_fusion.2
  71.1 22.6 %all-to-all-done.5 = bf16[4,512,512]{2,1,0:T(8,128)(2,1)} async-done(((bf16[4,512,512]{2,1,0:T(8,128)(2,1)}), bf16[4,512,512]{2,1,0:T(8,128)(2,1)}, u32[]{:S(2)}, u32[]{:S(2)}) %all-to-all-start.5) | async-done | bytes 2097184 | tf_op jit(solution)/shard_map/all_to_all | solution.py:139
  93.7 4.5 %all-to-all-start.3 = ((bf16[4,512,512]{2,1,0:T(8,128)(2,1)}), bf16[4,512,512]{2,1,0:T(8,128)(2,1)}, u32[]{:S(2)}, u32[]{:S(2)}) async-start(bf16[4,512,512]{2,1,0:T(8,128)(2,1)} %pad_maximum_fusion.2), calls=%async_computation.3 | async-start | bytes 4194304 | tf_op jit(solution)/shard_map/all_to_all | solution.py:139
  100.3 5.1 %collective-permute-start = (bf16[2,896,256]{2,1,0:T(8,128)(2,1)}, bf16[2,896,256]{2,1,0:T(8,128)(2,1)}, u32[]{:S(2)}, u32[]{:S(2)}) collective-permute-start(bf16[2,896,256]{2,1,0:T(8,128)(2,1)} %slice.118), channel_id=1, source_target_pairs={{0,4},{4,8},{8,12},{12,16},{16,20},{20,24},{24,28},{1,5},{5,9},{9,... | collective-permute-start | bytes 2752520 | tf_op jit(solution)/shard_map/ppermute | solution.py:123
  106.5 1.6 pad_maximum_fusion
  108.0 15.9 %all-to-all-done.3 = bf16[4,512,512]{2,1,0:T(8,128)(2,1)} async-done(((bf16[4,512,512]{2,1,0:T(8,128)(2,1)}), bf16[4,512,512]{2,1,0:T(8,128)(2,1)}, u32[]{:S(2)}, u32[]{:S(2)}) %all-to-all-start.3) | async-done | bytes 2097184 | tf_op jit(solution)/shard_map/all_to_all | solution.py:139
  123.9 4.5 %all-to-all-start = ((bf16[4,512,512]{2,1,0:T(8,128)(2,1)}), bf16[4,512,512]{2,1,0:T(8,128)(2,1)}, u32[]{:S(2)}, u32[]{:S(2)}) async-start(bf16[4,512,512]{2,1,0:T(8,128)(2,1)} %pad_maximum_fusion), calls=%async_computation | async-start | bytes 4194304 | tf_op jit(solution)/shard_map/all_to_all | solution.py:139
  133.1 17.6 %attend.7 = bf16[16,128,512]{2,1,0:T(8,128)(2,1)} custom-call(s32[16]{0:T(128)} %reduce_sum.40.block_ref, s32[16]{0:T(128)} %select_reduce_fusion.count_ref, bf16[2048,512]{1,0:T(8,128)(2,1)} %bitcast.40.q_ref, bf16[2944,256]{1,0:T(8,128)(2,1)} %pad_maximum_fusion.5.k_ref, bf16[2944,256]{1,0:T(8,128)(2,1)} %pad_maximum_fusion.6.v_ref), custom_call_target="tpu_custom_call" | custom-call | flops 2684354560 | bytes 7208960 | tf_op jit(solution)/shard_map/attend/pallas_call | solution.py:67
  150.7 3.4 all-to-all-done
  154.1 6.6 %all-to-all-start.8 = ((bf16[16,128,512]{2,1,0:T(8,128)(2,1)}), bf16[16,128,512]{2,1,0:T(8,128)(2,1)S(1)}, u32[]{:S(2)}, u32[]{:S(2)}) async-start(bf16[16,128,512]{2,1,0:T(8,128)(2,1)} %attend.7), calls=%async_computation.8 | async-start | bytes 4194304 | tf_op jit(solution)/shard_map/all_to_all | solution.py:189
  160.7 17.6 %attend.6 = bf16[16,128,512]{2,1,0:T(8,128)(2,1)} custom-call(s32[16]{0:T(128)} %reduce_sum.40.block_ref, s32[16]{0:T(128)} %select_reduce_fusion.count_ref, bf16[2048,512]{1,0:T(8,128)(2,1)} %bitcast.35.q_ref, bf16[2944,256]{1,0:T(8,128)(2,1)} %pad_maximum_fusion.5.k_ref, bf16[2944,256]{1,0:T(8,128)(2,1)} %pad_maximum_fusion.6.v_ref), custom_call_target="tpu_custom_call" | custom-call | flops 2684354560 | bytes 7208960 | tf_op jit(solution)/shard_map/attend/pallas_call | solution.py:67
  178.3 30.3 %all-to-all-done.8.x_ref = bf16[16,128,512]{2,1,0:T(8,128)(2,1)S(1)} async-done(((bf16[16,128,512]{2,1,0:T(8,128)(2,1)}), bf16[16,128,512]{2,1,0:T(8,128)(2,1)S(1)}, u32[]{:S(2)}, u32[]{:S(2)}) %all-to-all-start.8) | async-done | bytes 2097184 | tf_op jit(solution)/shard_map/all_to_all | solution.py:189
  209.9 4.5 %all-to-all-start.6 = ((bf16[16,128,512]{2,1,0:T(8,128)(2,1)}), bf16[16,128,512]{2,1,0:T(8,128)(2,1)}, u32[]{:S(2)}, u32[]{:S(2)}) async-start(bf16[16,128,512]{2,1,0:T(8,128)(2,1)} %attend.6), calls=%async_computation.6 | async-start | bytes 4194304 | tf_op jit(solution)/shard_map/all_to_all | solution.py:189
  214.5 17.6 %attend.5 = bf16[16,128,512]{2,1,0:T(8,128)(2,1)} custom-call(s32[16]{0:T(128)} %reduce_sum.40.block_ref, s32[16]{0:T(128)} %select_reduce_fusion.count_ref, bf16[2048,512]{1,0:T(8,128)(2,1)} %bitcast.30.q_ref, bf16[2944,256]{1,0:T(8,128)(2,1)} %pad_maximum_fusion.5.k_ref, bf16[2944,256]{1,0:T(8,128)(2,1)} %pad_maximum_fusion.6.v_ref), custom_call_target="tpu_custom_call" | custom-call | flops 2684354560 | bytes 7208960 | tf_op jit(solution)/shard_map/attend/pallas_call | solution.py:67
  232.1 30.1 %all-to-all-done.6.x_ref = bf16[16,128,512]{2,1,0:T(8,128)(2,1)} async-done(((bf16[16,128,512]{2,1,0:T(8,128)(2,1)}), bf16[16,128,512]{2,1,0:T(8,128)(2,1)}, u32[]{:S(2)}, u32[]{:S(2)}) %all-to-all-start.6) | async-done | bytes 2097184 | tf_op jit(solution)/shard_map/all_to_all | solution.py:189
  262.2 3.6 all-to-all-start.4
  265.8 17.6 %attend.4 = bf16[16,128,512]{2,1,0:T(8,128)(2,1)} custom-call(s32[16]{0:T(128)} %reduce_sum.40.block_ref, s32[16]{0:T(128)} %select_reduce_fusion.count_ref, bf16[2048,512]{1,0:T(8,128)(2,1)} %bitcast.7.q_ref, bf16[2944,256]{1,0:T(8,128)(2,1)} %pad_maximum_fusion.5.k_ref, bf16[2944,256]{1,0:T(8,128)(2,1)} %pad_maximum_fusion.6.v_ref), custom_call_target="tpu_custom_call" | custom-call | flops 2684354560 | bytes 7208960 | tf_op jit(solution)/shard_map/attend/pallas_call | solution.py:67
  283.4 30.7 %all-to-all-done.4.x_ref = bf16[16,128,512]{2,1,0:T(8,128)(2,1)S(1)} async-done(((bf16[16,128,512]{2,1,0:T(8,128)(2,1)}), bf16[16,128,512]{2,1,0:T(8,128)(2,1)S(1)}, u32[]{:S(2)}, u32[]{:S(2)}) %all-to-all-start.4) | async-done | bytes 2097184 | tf_op jit(solution)/shard_map/all_to_all | solution.py:189
  315.6 4.4 %all-to-all-start.2 = ((bf16[16,128,512]{2,1,0:T(8,128)(2,1)}), bf16[16,128,512]{2,1,0:T(8,128)(2,1)}, u32[]{:S(2)}, u32[]{:S(2)}) async-start(bf16[16,128,512]{2,1,0:T(8,128)(2,1)} %attend.4), calls=%async_computation.2 | async-start | bytes 4194304 | tf_op jit(solution)/shard_map/all_to_all | solution.py:189
  320.5 10.1 %place.4.rest_0_ = bf16[2048,2048]{1,0:T(8,128)(2,1)} custom-call(s32[16]{0:T(128)} %dynamic-slice_bitcast_fusion.slot_ref, bf16[16,128,512]{2,1,0:T(8,128)(2,1)} %copy-done), custom_call_target="tpu_custom_call" | custom-call | bytes 4194304 | tf_op jit(solution)/shard_map/place/pallas_call | solution.py:102
  330.7 10.1 %place.5.rest_0_ = bf16[2048,2048]{1,0:T(8,128)(2,1)} custom-call(s32[16]{0:T(128)} %dynamic-slice_bitcast_fusion.slot_ref, bf16[16,128,512]{2,1,0:T(8,128)(2,1)} %all-to-all-done.6.x_ref, bf16[2048,2048]{1,0:T(8,128)(2,1)} %place.4.rest_0_), custom_call_target="tpu_custom_call", output_to_operand_aliasing={{}: (2, {})} | custom-call | bytes 4194304 | tf_op jit(solution)/shard_map/place/pallas_call | solution.py:102
  340.8 10.1 %place.6.rest_0_ = bf16[2048,2048]{1,0:T(8,128)(2,1)} custom-call(s32[16]{0:T(128)} %dynamic-slice_bitcast_fusion.slot_ref, bf16[16,128,512]{2,1,0:T(8,128)(2,1)} %copy-done.1, bf16[2048,2048]{1,0:T(8,128)(2,1)} %place.5.rest_0_), custom_call_target="tpu_custom_call", output_to_operand_aliasing={{}: (2, {})} | custom-call | bytes 4194304 | tf_op jit(solution)/shard_map/place/pallas_call | solution.py:102
  351.0 16.7 %all-to-all-done.2.x_ref = bf16[16,128,512]{2,1,0:T(8,128)(2,1)} async-done(((bf16[16,128,512]{2,1,0:T(8,128)(2,1)}), bf16[16,128,512]{2,1,0:T(8,128)(2,1)}, u32[]{:S(2)}, u32[]{:S(2)}) %all-to-all-start.2) | async-done | bytes 2097184 | tf_op jit(solution)/shard_map/all_to_all | solution.py:189
  367.7 10.1 %place.7 = bf16[2048,2048]{1,0:T(8,128)(2,1)} custom-call(s32[16]{0:T(128)} %dynamic-slice_bitcast_fusion.slot_ref, bf16[16,128,512]{2,1,0:T(8,128)(2,1)} %all-to-all-done.2.x_ref, bf16[2048,2048]{1,0:T(8,128)(2,1)} %place.6.rest_0_), custom_call_target="tpu_custom_call", output_to_operand_aliasing={{}: (2, {})} | custom-call | bytes 4194304 | tf_op jit(solution)/shard_map/place/pallas_call | solution.py:102
  (46 shorter events, 14.4 us)
Async XLA Ops:
  0.0 1.6 copy-start.4
  3.4 29.9 %all-to-all-start.1 = ((bf16[4,2,512,256]{3,2,1,0:T(8,128)(2,1)}), bf16[4,2,512,256]{3,2,1,0:T(8,128)(2,1)S(1)}, u32[]{:S(2)}, u32[]{:S(2)}) async-start(bf16[4,2,512,256]{3,2,1,0:T(8,128)(2,1)} %pad_maximum_fusion.1), calls=%async_computation.1 | async-start | bytes 4194304 | tf_op jit(solution)/shard_map/all_to_all | solution.py:139
  33.4 30.2 %all-to-all-start.7 = ((bf16[4,512,512]{2,1,0:T(8,128)(2,1)}), bf16[4,512,512]{2,1,0:T(8,128)(2,1)}, u32[]{:S(2)}, u32[]{:S(2)}) async-start(bf16[4,512,512]{2,1,0:T(8,128)(2,1)} %pad_maximum_fusion.4), calls=%async_computation.7 | async-start | bytes 4194304 | tf_op jit(solution)/shard_map/all_to_all | solution.py:139
  63.5 30.2 %all-to-all-start.5 = ((bf16[4,512,512]{2,1,0:T(8,128)(2,1)}), bf16[4,512,512]{2,1,0:T(8,128)(2,1)}, u32[]{:S(2)}, u32[]{:S(2)}) async-start(bf16[4,512,512]{2,1,0:T(8,128)(2,1)} %pad_maximum_fusion.3), calls=%async_computation.5 | async-start | bytes 4194304 | tf_op jit(solution)/shard_map/all_to_all | solution.py:139
  71.1 27.1 %copy-start.5 = (s32[128]{0:T(128)S(1)}, s32[128]{0:T(128)}, u32[]{:S(2)}) copy-start(s32[128]{0:T(128)} %param.9) | copy-start | bytes 1540
  71.1 27.3 %copy-start.6 = (s32[128]{0:T(128)S(1)}, s32[128]{0:T(128)}, u32[]{:S(2)}) copy-start(s32[128]{0:T(128)} %param.8) | copy-start | bytes 1540
  93.7 30.2 %all-to-all-start.3 = ((bf16[4,512,512]{2,1,0:T(8,128)(2,1)}), bf16[4,512,512]{2,1,0:T(8,128)(2,1)}, u32[]{:S(2)}, u32[]{:S(2)}) async-start(bf16[4,512,512]{2,1,0:T(8,128)(2,1)} %pad_maximum_fusion.2), calls=%async_computation.3 | async-start | bytes 4194304 | tf_op jit(solution)/shard_map/all_to_all | solution.py:139
  99.1 7.4 %copy-start.2 = (bf16[1,512,512]{2,1,0:T(8,128)(2,1)S(1)}, bf16[1,512,512]{2,1,0:T(8,128)(2,1)}, u32[]{:S(2)}) copy-start(bf16[1,512,512]{2,1,0:T(8,128)(2,1)} %get-tuple-element.19) | copy-start | bytes 1572868
  99.1 7.4 %copy-start.3 = (bf16[1,512,512]{2,1,0:T(8,128)(2,1)S(1)}, bf16[1,512,512]{2,1,0:T(8,128)(2,1)}, u32[]{:S(2)}) copy-start(bf16[1,512,512]{2,1,0:T(8,128)(2,1)} %get-tuple-element.20) | copy-start | bytes 1572868
  100.3 29.0 %collective-permute-start = (bf16[2,896,256]{2,1,0:T(8,128)(2,1)}, bf16[2,896,256]{2,1,0:T(8,128)(2,1)}, u32[]{:S(2)}, u32[]{:S(2)}) collective-permute-start(bf16[2,896,256]{2,1,0:T(8,128)(2,1)} %slice.118), channel_id=1, source_target_pairs={{0,4},{4,8},{8,12},{12,16},{16,20},{20,24},{24,28},{1,5},{5,9},{9,... | collective-permute-start | bytes 2752520 | tf_op jit(solution)/shard_map/ppermute | solution.py:123
  123.9 30.2 %all-to-all-start = ((bf16[4,512,512]{2,1,0:T(8,128)(2,1)}), bf16[4,512,512]{2,1,0:T(8,128)(2,1)}, u32[]{:S(2)}, u32[]{:S(2)}) async-start(bf16[4,512,512]{2,1,0:T(8,128)(2,1)} %pad_maximum_fusion), calls=%async_computation | async-start | bytes 4194304 | tf_op jit(solution)/shard_map/all_to_all | solution.py:139
  154.1 54.5 %all-to-all-start.8 = ((bf16[16,128,512]{2,1,0:T(8,128)(2,1)}), bf16[16,128,512]{2,1,0:T(8,128)(2,1)S(1)}, u32[]{:S(2)}, u32[]{:S(2)}) async-start(bf16[16,128,512]{2,1,0:T(8,128)(2,1)} %attend.7), calls=%async_computation.8 | async-start | bytes 4194304 | tf_op jit(solution)/shard_map/all_to_all | solution.py:189
  208.6 1.3 copy-start
  209.9 52.3 %all-to-all-start.6 = ((bf16[16,128,512]{2,1,0:T(8,128)(2,1)}), bf16[16,128,512]{2,1,0:T(8,128)(2,1)}, u32[]{:S(2)}, u32[]{:S(2)}) async-start(bf16[16,128,512]{2,1,0:T(8,128)(2,1)} %attend.6), calls=%async_computation.6 | async-start | bytes 4194304 | tf_op jit(solution)/shard_map/all_to_all | solution.py:189
  262.2 52.0 %all-to-all-start.4 = ((bf16[16,128,512]{2,1,0:T(8,128)(2,1)}), bf16[16,128,512]{2,1,0:T(8,128)(2,1)S(1)}, u32[]{:S(2)}, u32[]{:S(2)}) async-start(bf16[16,128,512]{2,1,0:T(8,128)(2,1)} %attend.5), calls=%async_computation.4 | async-start | bytes 4194304 | tf_op jit(solution)/shard_map/all_to_all | solution.py:189
  314.2 1.4 copy-start.1
  315.6 52.2 %all-to-all-start.2 = ((bf16[16,128,512]{2,1,0:T(8,128)(2,1)}), bf16[16,128,512]{2,1,0:T(8,128)(2,1)}, u32[]{:S(2)}, u32[]{:S(2)}) async-start(bf16[16,128,512]{2,1,0:T(8,128)(2,1)} %attend.4), calls=%async_computation.2 | async-start | bytes 4194304 | tf_op jit(solution)/shard_map/all_to_all | solution.py:189
